TPU v7x, 32 devices: a whole 2x2x4 slice. The times are simulated.
32 devices in a mesh: row: 8 (over z, y), col: 4 (over x, core).
Axes of the slice: x: 2, y: 2, z: 4, core: 2. Of those that a mesh axis runs over, the one named last changes fastest.
Arguments:
- signal: bfloat16 [8, 256, 512], P(None, 'row', 'col'), may hold values from -6 to 6
- filter_real: bfloat16 [8, 256, 512], P(None, 'row', 'col'), may hold values from -6 to 6
- filter_imag: bfloat16 [8, 256, 512], P(None, 'row', 'col'), may hold values from -6 to 6
- skip: float32 [8], replicated, may hold values from 0.5 to 1.5
Outputs:
- output: bfloat16 [8, 256, 512], P(None, 'row', 'col')
All inputs are finite; a program needn't handle non-finite values.
Results may differ from a plain program's by a relative error of at most 0.0064.
Values may be sent and summed in bfloat16 or wider, within the bound.
No kernel may reach another device: no remote copies, remote signals or barrier semaphores. Data moves between devices by JAX's collectives and lax.ppermute only.
A program may use at most 64 MiB of HBM per device.

v0:
```python
import math
import jax
import jax.numpy as jnp
from jax import lax
from jax.sharding import PartitionSpec as P


def phase_table(left_ids, right_ids, modulus):
    product = left_ids[:, None] * right_ids[None, :] % modulus
    angle = -2.0 * math.pi / modulus * product.astype(jnp.float32)
    return (jnp.cos(angle).astype(jnp.bfloat16), jnp.sin(angle).astype(jnp.bfloat16))


def twist_table(left_ids, right_ids, modulus):
    product = left_ids[:, None] * right_ids[None, :] % modulus
    angle = -2.0 * math.pi / modulus * product.astype(jnp.float32)
    return (jnp.cos(angle), jnp.sin(angle))


def column_product(series, phase):
    return jnp.einsum("crn,nk->crk", series, phase, preferred_element_type=jnp.float32)


def row_product(phase, series):
    return jnp.einsum("rn,cnj->crj", phase, series, preferred_element_type=jnp.float32)


def local(signal, filter_real, filter_imag, skip):
    channels, row_count, col_count = signal.shape
    first_len = row_count * lax.axis_size("row")
    second_len = col_count * lax.axis_size("col")
    seq_len = first_len * second_len
    row_offset = lax.axis_index("row") * row_count
    col_offset = lax.axis_index("col") * col_count
    own_rows = row_offset + jnp.arange(row_count, dtype=jnp.int32)
    own_cols = col_offset + jnp.arange(col_count, dtype=jnp.int32)
    twist_re, twist_im = twist_table(own_rows, own_cols, seq_len)
    pair_width = col_count // lax.axis_size("row")
    pair_cols = (
        col_offset + lax.axis_index("row") * pair_width + jnp.arange(pair_width, dtype=jnp.int32)
    )
    all_rows = jnp.arange(first_len, dtype=jnp.int32)
    full_re, full_im = phase_table(all_rows, all_rows, first_len)
    columns_whole = lax.all_to_all(signal, "row", split_axis=2, concat_axis=1, tiled=True)
    pair_b_re = row_product(full_re, columns_whole)
    pair_b_im = row_product(full_im, columns_whole)
    pair_tw_re, pair_tw_im = twist_table(all_rows, pair_cols, seq_len)
    pair_mix_re = (pair_b_re * pair_tw_re - pair_b_im * pair_tw_im).astype(jnp.bfloat16)
    pair_mix_im = (pair_b_re * pair_tw_im + pair_b_im * pair_tw_re).astype(jnp.bfloat16)
    mixed_re, mixed_im = (
        lax.all_to_all(pair_mix_re, "row", split_axis=1, concat_axis=2, tiled=True),
        lax.all_to_all(pair_mix_im, "row", split_axis=1, concat_axis=2, tiled=True),
    )
    pieces = (
        lax.all_gather(mixed_re, "col", axis=2, tiled=True),
        lax.all_gather(mixed_im, "col", axis=2, tiled=True),
    )
    amount = pieces[0].shape[2]
    phase_re, phase_im = phase_table(jnp.arange(amount, dtype=jnp.int32), own_cols, second_len)
    part_re, part_im = pieces
    new_re = column_product(part_re, phase_re) - column_product(part_im, phase_im)
    new_im = column_product(part_re, phase_im) + column_product(part_im, phase_re)
    spec_re = new_re
    spec_im = new_im
    prod_re = (spec_re * filter_real - spec_im * filter_imag).astype(jnp.bfloat16)
    prod_im = (spec_re * filter_imag + spec_im * filter_real).astype(jnp.bfloat16)
    pieces = (
        lax.all_gather(prod_re, "col", axis=2, tiled=True),
        lax.all_gather(prod_im, "col", axis=2, tiled=True),
    )
    amount = pieces[0].shape[2]
    phase_re, phase_im = phase_table(jnp.arange(amount, dtype=jnp.int32), own_cols, second_len)
    part_re, part_im = pieces
    new_re = column_product(part_re, phase_re) + column_product(part_im, phase_im)
    new_im = column_product(part_im, phase_re) - column_product(part_re, phase_im)
    unwound_re = (new_re * twist_re + new_im * twist_im).astype(jnp.bfloat16)
    unwound_im = (new_im * twist_re - new_re * twist_im).astype(jnp.bfloat16)
    pair_un_re, pair_un_im = (
        lax.all_to_all(unwound_re, "row", split_axis=2, concat_axis=1, tiled=True),
        lax.all_to_all(unwound_im, "row", split_axis=2, concat_axis=1, tiled=True),
    )
    pair_total = row_product(full_re, pair_un_re) + row_product(full_im, pair_un_im)
    pair_out = (
        pair_total / seq_len + skip[:, None, None] * columns_whole.astype(jnp.float32)
    ).astype(jnp.bfloat16)
    return lax.all_to_all(pair_out, "row", split_axis=1, concat_axis=2, tiled=True)


def solution(mesh):
    in_specs = (P(None, "row", "col"), P(None, "row", "col"), P(None, "row", "col"), P())
    out_specs = P(None, "row", "col")
    return jax.shard_map(local, mesh=mesh, in_specs=in_specs, out_specs=out_specs, check_vma=False)
```

profile of v0, /device:TPU:0, one launch (start us, length us, event | category | flops | bytes accessed | tf_op | source)
XLA Modules:
  0.0 107.6 jit_solution(13827530816031073000)
XLA Ops:
  0.0 1.0 copy.23
  1.0 0.9 reshape.142
  1.9 7.3 %all-to-all-start = ((bf16[8,2,2048]{2,1,0:T(2,128)(2,1)}), bf16[8,2,2048]{2,1,0:T(2,128)(2,1)S(1)}, u32[]{:S(2)}, u32[]{:S(2)}) async-start(bf16[8,2,2048]{2,1,0:T(2,128)(2,1)} %reshape.142), calls=%async_computation | async-start | bytes 131072 | tf_op jit(solution)/shard_map/all_to_all | solution.py:44
  9.4 6.7 %all-to-all-done = bf16[8,2,2048]{2,1,0:T(2,128)(2,1)S(1)} async-done(((bf16[8,2,2048]{2,1,0:T(2,128)(2,1)}), bf16[8,2,2048]{2,1,0:T(2,128)(2,1)S(1)}, u32[]{:S(2)}, u32[]{:S(2)}) %all-to-all-start) | async-done | bytes 65568 | tf_op jit(solution)/shard_map/all_to_all | solution.py:44
  16.2 0.2 reshape.143
  16.7 1.1 %fusion.38 = f32[256,128]{0,1:S(1)} fusion(bf16[256,128]{0,1:T(8,128)(2,1)S(1)} %bitcast.113), kind=kOutput, calls=%fused_computation.53 | convolution fusion | flops 17760256 | bytes 196608
  17.8 1.1 %fusion.37 = f32[256,128]{0,1:S(1)} fusion(bf16[256,128]{0,1:T(8,128)(2,1)S(1)} %bitcast.114), kind=kOutput, calls=%fused_computation.52 | convolution fusion | flops 17760256 | bytes 196608
  19.0 0.3 copy.26
  19.3 1.2 %reshape.144 = bf16[8,2,2048]{2,1,0:T(2,128)(2,1)} reshape(bf16[256,8,16]{2,1,0:T(8,128)(2,1)S(1)} %bitcast.96) | data formatting | bytes 131072
  20.5 3.4 %all-to-all-start.1 = ((bf16[8,2,2048]{2,1,0:T(2,128)(2,1)}), bf16[8,2,2048]{2,1,0:T(2,128)(2,1)S(1)}, u32[]{:S(2)}, u32[]{:S(2)}) async-start(bf16[8,2,2048]{2,1,0:T(2,128)(2,1)} %reshape.144), calls=%async_computation.1 | async-start | bytes 131072 | tf_op jit(solution)/shard_map/all_to_all | solution.py:51
  24.0 0.3 copy.29
  24.3 1.2 %reshape.146 = bf16[8,2,2048]{2,1,0:T(2,128)(2,1)} reshape(bf16[256,8,16]{2,1,0:T(8,128)(2,1)S(1)} %bitcast.97) | data formatting | bytes 131072
  25.5 5.2 %all-to-all-done.1 = bf16[8,2,2048]{2,1,0:T(2,128)(2,1)S(1)} async-done(((bf16[8,2,2048]{2,1,0:T(2,128)(2,1)}), bf16[8,2,2048]{2,1,0:T(2,128)(2,1)S(1)}, u32[]{:S(2)}, u32[]{:S(2)}) %all-to-all-start.1) | async-done | bytes 65568 | tf_op jit(solution)/shard_map/all_to_all | solution.py:51
  30.7 3.3 %all-to-all-start.2 = ((bf16[8,2,2048]{2,1,0:T(2,128)(2,1)}), bf16[8,2,2048]{2,1,0:T(2,128)(2,1)S(1)}, u32[]{:S(2)}, u32[]{:S(2)}) async-start(bf16[8,2,2048]{2,1,0:T(2,128)(2,1)} %reshape.146), calls=%async_computation.2 | async-start | bytes 131072 | tf_op jit(solution)/shard_map/all_to_all | solution.py:52
  34.0 0.4 reshape.145
  34.4 0.4 copy.27
  34.9 5.8 %all_gather.12 = bf16[8,32,512]{2,1,0:T(8,128)(2,1)S(1)} all-gather(bf16[8,32,128]{2,1,0:T(8,128)(2,1)S(1)} %copy.28), channel_id=1, replica_groups=mesh['row'=8,'col'=4] {'col'}, dimensions={2}, use_global_device_ids=true | all-gather | bytes 327680 | tf_op jit(solution)/shard_map/all_gather | solution.py:55
  40.8 1.2 %fusion.27 = f32[8,32,128]{2,1,0:T(8,128)S(1)} fusion(bf16[8,32,512]{2,1,0:T(8,128)(2,1)S(1)} %all_gather.12, s32[128]{0:T(128)S(1)} %iota_add_fusion.1), kind=kOutput, calls=%fused_computation.47 | convolution fusion | flops 34537472 | bytes 393728 | tf_op jit(solution)/shard_map/crn,nk->crk/dot_general | solution.py:21
  41.9 1.2 %fusion.35 = f32[8,32,128]{2,1,0:T(8,128)S(1)} fusion(bf16[8,32,512]{2,1,0:T(8,128)(2,1)S(1)} %all_gather.12, s32[128]{0:T(128)S(1)} %iota_add_fusion.1), kind=kOutput, calls=%fused_computation.50 | convolution fusion | flops 34537472 | bytes 393728 | tf_op jit(solution)/shard_map/crn,nk->crk/dot_general | solution.py:21
  43.1 0.4 reshape.147
  43.5 0.4 copy.30
  44.0 5.9 %all_gather.13 = bf16[8,32,512]{2,1,0:T(8,128)(2,1)S(1)} all-gather(bf16[8,32,128]{2,1,0:T(8,128)(2,1)S(1)} %copy.31), channel_id=1, replica_groups=mesh['row'=8,'col'=4] {'col'}, dimensions={2}, use_global_device_ids=true | all-gather | bytes 327680 | tf_op jit(solution)/shard_map/all_gather | solution.py:56
  49.9 1.2 %convolution_add_fusion.1 = f32[8,32,128]{2,1,0:T(8,128)S(1)} fusion(f32[8,32,128]{2,1,0:T(8,128)S(1)} %fusion.27, bf16[8,32,512]{2,1,0:T(8,128)(2,1)S(1)} %all_gather.13, s32[128]{0:T(128)S(1)} %iota_add_fusion.1), kind=kOutput, calls=%fused_computation.2 | convolution fusion | flops 34570240 | bytes 524800 | tf_op jit(solution)/shard_map/crn,nk->crk/dot_general | solution.py:21
  51.1 1.2 %fusion.17 = (bf16[8,32,128]{2,1,0:T(8,128)(2,1)S(1)}, bf16[8,32,128]{2,1,0:T(8,128)(2,1)S(1)}) fusion(bf16[8,32,128]{2,1,0:T(8,128)(2,1)S(1)} %copy-done, f32[8,32,128]{2,1,0:T(8,128)S(1)} %convolution_add_fusion.1, bf16[8,32,128]{2,1,0:T(8,128)(2,1)S(1)} %copy-done.1, f32[8,32,128]{2,1,0:T(8,128)S(1)} %fusion.35, bf16[8,32,512]{2,1,0:T(8,128)(2,1)S(1)} %all_gather.13, ...), kind=kOutput, calls=%fused_computation.36 | convolution fusion | flops 34897920 | bytes 786944 | tf_op jit(solution)/shard_map/crn,nk->crk/dot_general | solution.py:21
  52.3 6.1 %all_gather.14 = bf16[8,32,512]{2,1,0:T(8,128)(2,1)S(1)} all-gather(bf16[8,32,128]{2,1,0:T(8,128)(2,1)S(1)} %get-tuple-element.5), channel_id=1, replica_groups=mesh['row'=8,'col'=4] {'col'}, dimensions={2}, use_global_device_ids=true | all-gather | bytes 327680 | tf_op jit(solution)/shard_map/all_gather | solution.py:68
  58.4 1.2 %fusion.32 = f32[8,32,128]{2,1,0:T(8,128)S(1)} fusion(bf16[8,32,512]{2,1,0:T(8,128)(2,1)S(1)} %all_gather.14, s32[128]{0:T(128)S(1)} %iota_add_fusion.1), kind=kOutput, calls=%fused_computation.49 | convolution fusion | flops 34537472 | bytes 393728 | tf_op jit(solution)/shard_map/crn,nk->crk/dot_general | solution.py:21
  59.5 5.9 %all_gather.15 = bf16[8,32,512]{2,1,0:T(8,128)(2,1)S(1)} all-gather(bf16[8,32,128]{2,1,0:T(8,128)(2,1)S(1)} %get-tuple-element.6), channel_id=1, replica_groups=mesh['row'=8,'col'=4] {'col'}, dimensions={2}, use_global_device_ids=true | all-gather | bytes 327680 | tf_op jit(solution)/shard_map/all_gather | solution.py:69
  65.4 1.2 %fusion.30 = f32[8,32,128]{2,1,0:T(8,128)S(1)} fusion(bf16[8,32,512]{2,1,0:T(8,128)(2,1)S(1)} %all_gather.15, s32[128]{0:T(128)S(1)} %iota_add_fusion.1), kind=kOutput, calls=%fused_computation.48 | convolution fusion | flops 34537472 | bytes 393728 | tf_op jit(solution)/shard_map/crn,nk->crk/dot_general | solution.py:21
  66.6 1.2 %convolution_subtract_fusion = f32[8,32,128]{2,1,0:T(8,128)S(1)} fusion(f32[8,32,128]{2,1,0:T(8,128)S(1)} %fusion.30, bf16[8,32,512]{2,1,0:T(8,128)(2,1)S(1)} %all_gather.14, s32[128]{0:T(128)S(1)} %iota_add_fusion.1), kind=kOutput, calls=%fused_computation | convolution fusion | flops 34570240 | bytes 524800 | tf_op jit(solution)/shard_map/crn,nk->crk/dot_general | solution.py:21
  67.8 1.2 %subtract_convert_fusion = (bf16[8,32,128]{2,1,0:T(8,128)(2,1)S(1)}, bf16[8,32,128]{2,1,0:T(8,128)(2,1)S(1)}) fusion(f32[8,32,128]{2,1,0:T(8,128)S(1)} %convolution_subtract_fusion, f32[32,128]{1,0:T(8,128)S(1)} %get-tuple-element.12, f32[32,128]{1,0:T(8,128)S(1)} %get-tuple-element.11, f32[8,32,128]{2,1,0:T(8,128)S(1)} %fusion.32, ...), kind=kOutput, calls=%fused_computation.44 | convolution fusion | flops 34832384 | bytes 688640 | tf_op jit(solution)/shard_map/crn,nk->crk/dot_general | solution.py:21
  68.9 0.2 copy.35
  69.1 0.9 reshape.150
  70.1 5.9 %all-to-all-start.4 = ((bf16[8,2,2048]{2,1,0:T(2,128)(2,1)}), bf16[8,2,2048]{2,1,0:T(2,128)(2,1)S(1)}, u32[]{:S(2)}, u32[]{:S(2)}) async-start(bf16[8,2,2048]{2,1,0:T(2,128)(2,1)} %reshape.150), calls=%async_computation.4 | async-start | bytes 131072 | tf_op jit(solution)/shard_map/all_to_all | solution.py:80
  76.0 0.2 copy.32
  76.2 0.9 reshape.148
  77.1 5.8 %all-to-all-done.4 = bf16[8,2,2048]{2,1,0:T(2,128)(2,1)S(1)} async-done(((bf16[8,2,2048]{2,1,0:T(2,128)(2,1)}), bf16[8,2,2048]{2,1,0:T(2,128)(2,1)S(1)}, u32[]{:S(2)}, u32[]{:S(2)}) %all-to-all-start.4) | async-done | bytes 65568 | tf_op jit(solution)/shard_map/all_to_all | solution.py:80
  82.9 3.4 %all-to-all-start.3 = ((bf16[8,2,2048]{2,1,0:T(2,128)(2,1)}), bf16[8,2,2048]{2,1,0:T(2,128)(2,1)S(1)}, u32[]{:S(2)}, u32[]{:S(2)}) async-start(bf16[8,2,2048]{2,1,0:T(2,128)(2,1)} %reshape.148), calls=%async_computation.3 | async-start | bytes 131072 | tf_op jit(solution)/shard_map/all_to_all | solution.py:79
  86.3 0.2 reshape.151
  86.8 6.3 %all-to-all-done.3 = bf16[8,2,2048]{2,1,0:T(2,128)(2,1)S(1)} async-done(((bf16[8,2,2048]{2,1,0:T(2,128)(2,1)}), bf16[8,2,2048]{2,1,0:T(2,128)(2,1)S(1)}, u32[]{:S(2)}, u32[]{:S(2)}) %all-to-all-start.3) | async-done | bytes 65568 | tf_op jit(solution)/shard_map/all_to_all | solution.py:79
  93.1 0.2 reshape.149
  93.7 1.1 %fusion.23 = f32[8,16,256]{2,1,0:T(8,128)S(1)} fusion(bf16[8,256,16]{1,2,0:T(8,128)(2,1)S(1)} %all_to_all.93), kind=kOutput, calls=%fused_computation.42 | convolution fusion | flops 17760256 | bytes 196608 | tf_op jit(solution)/shard_map/rn,cnj->crj/dot_general | solution.py:25
  94.8 1.1 %fusion.3 = bf16[8,256,16]{1,2,0:T(8,128)(2,1)S(1)} fusion(f32[8,16,256]{2,1,0:T(8,128)S(1)} %fusion.23, bf16[8,256,16]{1,2,0:T(8,128)(2,1)S(1)} %all_to_all.97, bf16[8,256,16]{1,2,0:T(8,128)(2,1)S(1)} %all_to_all.81, f32[8]{0:T(128)S(1)} %copy-done.2), kind=kOutput, calls=%fused_computation.8 | convolution fusion | flops 17956864 | bytes 327712 | tf_op jit(solution)/shard_map/rn,cnj->crj/dot_general | solution.py:25
  95.9 0.3 copy.38
  96.2 0.5 reshape.152
  96.8 9.3 %all_to_all.108 = bf16[8,2,2048]{2,1,0:T(2,128)(2,1)S(1)} all-to-all(bf16[8,2,2048]{2,1,0:T(2,128)(2,1)S(1)} %reshape.152), channel_id=1, replica_groups=mesh['row'=8,'col'=4] {'row'}, dimensions={0} | all-to-all | bytes 131072 | tf_op jit(solution)/shard_map/all_to_all | solution.py:86
  106.1 0.4 reshape.153
  106.4 0.4 copy.39
  106.8 0.8 copy.40
  (21 shorter events, 1.7 us)
Async XLA Ops:
  1.9 14.2 %all-to-all-start = ((bf16[8,2,2048]{2,1,0:T(2,128)(2,1)}), bf16[8,2,2048]{2,1,0:T(2,128)(2,1)S(1)}, u32[]{:S(2)}, u32[]{:S(2)}) async-start(bf16[8,2,2048]{2,1,0:T(2,128)(2,1)} %reshape.142), calls=%async_computation | async-start | bytes 131072 | tf_op jit(solution)/shard_map/all_to_all | solution.py:44
  20.5 10.2 %all-to-all-start.1 = ((bf16[8,2,2048]{2,1,0:T(2,128)(2,1)}), bf16[8,2,2048]{2,1,0:T(2,128)(2,1)S(1)}, u32[]{:S(2)}, u32[]{:S(2)}) async-start(bf16[8,2,2048]{2,1,0:T(2,128)(2,1)} %reshape.144), calls=%async_computation.1 | async-start | bytes 131072 | tf_op jit(solution)/shard_map/all_to_all | solution.py:51
  30.7 12.4 %all-to-all-start.2 = ((bf16[8,2,2048]{2,1,0:T(2,128)(2,1)}), bf16[8,2,2048]{2,1,0:T(2,128)(2,1)S(1)}, u32[]{:S(2)}, u32[]{:S(2)}) async-start(bf16[8,2,2048]{2,1,0:T(2,128)(2,1)} %reshape.146), calls=%async_computation.2 | async-start | bytes 131072 | tf_op jit(solution)/shard_map/all_to_all | solution.py:52
  49.9 1.2 %copy-start = (bf16[8,32,128]{2,1,0:T(8,128)(2,1)S(1)}, bf16[8,32,128]{2,1,0:T(8,128)(2,1)}, u32[]{:S(2)}) copy-start(bf16[8,32,128]{2,1,0:T(8,128)(2,1)} %param.5) | copy-start | bytes 196612
  49.9 1.2 %copy-start.1 = (bf16[8,32,128]{2,1,0:T(8,128)(2,1)S(1)}, bf16[8,32,128]{2,1,0:T(8,128)(2,1)}, u32[]{:S(2)}) copy-start(bf16[8,32,128]{2,1,0:T(8,128)(2,1)} %param.6) | copy-start | bytes 196612
  70.1 12.8 %all-to-all-start.4 = ((bf16[8,2,2048]{2,1,0:T(2,128)(2,1)}), bf16[8,2,2048]{2,1,0:T(2,128)(2,1)S(1)}, u32[]{:S(2)}, u32[]{:S(2)}) async-start(bf16[8,2,2048]{2,1,0:T(2,128)(2,1)} %reshape.150), calls=%async_computation.4 | async-start | bytes 131072 | tf_op jit(solution)/shard_map/all_to_all | solution.py:80
  82.9 10.2 %all-to-all-start.3 = ((bf16[8,2,2048]{2,1,0:T(2,128)(2,1)}), bf16[8,2,2048]{2,1,0:T(2,128)(2,1)S(1)}, u32[]{:S(2)}, u32[]{:S(2)}) async-start(bf16[8,2,2048]{2,1,0:T(2,128)(2,1)} %reshape.148), calls=%async_computation.3 | async-start | bytes 131072 | tf_op jit(solution)/shard_map/all_to_all | solution.py:79
  93.6 1.1 %copy-start.2 = (f32[8]{0:T(128)S(1)}, f32[8]{0:T(128)}, u32[]{:S(2)}) copy-start(f32[8]{0:T(128)} %param.7) | copy-start | bytes 100
where the time goes:
time: 108 us
  blocking collectives  33 us (31%)
  waiting for transfers between devices  24 us (22%)
  starting transfers between devices  23.3 us (22%)
  matrix products  13.7 us (13%)
  local copies, waits for them, and re-layouts  12.9 us (12%)
    all_to_all x1, blocking collectives, local(): lax.all_to_all(pair_out, 'row', split_axis=1, concat_axis=2, tiled=True)  9.29 us
    dot_general x8, matrix products, column_product(): jnp.einsum('crn,nk->crk', series, phase, preferred_element_type=jnp.float32)  9.28 us
    unnamed x19, local copies, waits for them, and re-layouts  8.34 us
    all_to_all x1, starting transfers between devices, local(): lax.all_to_all(signal, 'row', split_axis=2, concat_axis=1, tiled=True)  7.31 us
    all_to_all x1, waiting for transfers between devices, local(): lax.all_to_all(signal, 'row', split_axis=2, concat_axis=1, tiled=True)  6.72 us
    all_to_all x1, waiting for transfers between devices, local(): lax.all_to_all(unwound_re, 'row', split_axis=2, concat_axis=1, tiled=True)  6.29 us
    all_gather x1, blocking collectives, local(): lax.all_gather(prod_re, 'col', axis=2, tiled=True)  6.09 us
    all_to_all x1, starting transfers between devices, local(): lax.all_to_all(unwound_im, 'row', split_axis=2, concat_axis=1, tiled=True)  5.93 us
  transfers between devices with their start and end apart: 5, of which 4 were waited for; matrix products, arithmetic and copies ran while one was open for 6% of the time, Pallas kernels for 0%

commit v1 on v0

--- a/solution.py
+++ b/solution.py
@@ -3,6 +3,22 @@
 import jax.numpy as jnp
 from jax import lax
 from jax.sharding import PartitionSpec as P
+
+
+def groups_create(axis_name, message):
+    everything, mid_arr = (lax.axis_size(axis_name), lax.axis_index(axis_name))
+    mixed_arr = message.shape[2] // everything
+    current_block = list(message.shape)
+    current_block[2] = mixed_arr
+    tmp = current_block[1]
+    current_block[1] = tmp * everything
+    y1 = jnp.zeros(current_block, message.dtype)
+    for h in range(everything):
+        a_next = lax.dynamic_slice_in_dim(message, (mid_arr ^ h) * mixed_arr, mixed_arr, axis=2)
+        if h:
+            a_next = lax.ppermute(a_next, axis_name, [(c, c ^ h) for c in range(everything)])
+        y1 = lax.dynamic_update_slice_in_dim(y1, a_next, (mid_arr ^ h) * tmp, axis=1)
+    return y1
 
 
 def phase_table(left_ids, right_ids, modulus):
@@ -41,7 +57,7 @@
     )
     all_rows = jnp.arange(first_len, dtype=jnp.int32)
     full_re, full_im = phase_table(all_rows, all_rows, first_len)
-    columns_whole = lax.all_to_all(signal, "row", split_axis=2, concat_axis=1, tiled=True)
+    columns_whole = groups_create("row", signal)
     pair_b_re = row_product(full_re, columns_whole)
     pair_b_im = row_product(full_im, columns_whole)
     pair_tw_re, pair_tw_im = twist_table(all_rows, pair_cols, seq_len)

time: 108 us -> 118 us (1.093)
  starting transfers between devices: 23.3 us -> 31.7 us
  local copies, waits for them, and re-layouts: 12.9 us -> 20.9 us
  waiting for transfers between devices: 24 us -> 17.1 us
    ppermute x0 -> x7, starting transfers between devices: none -> 12.9 us  [groups_create(): lax.ppermute(a_next, axis_name, [(c, c ^ h) for c in range(everything)])]
    dynamic_update_slice x0 -> x8, local copies, waits for them, and re-layouts: none -> 8.64 us  [groups_create(): lax.dynamic_update_slice_in_dim(y1, a_next, (mid_arr ^ h) * tmp, axis=1)]
    all_to_all x1 -> x0, starting transfers between devices: 7.31 us -> none  [local(): lax.all_to_all(signal, 'row', split_axis=2, concat_axis=1, tiled=True)]
    all_to_all x1 -> x0, waiting for transfers between devices: 6.72 us -> none  [local(): lax.all_to_all(signal, 'row', split_axis=2, concat_axis=1, tiled=True)]
    all_to_all x1, starting transfers between devices: 3.35 us -> 5.95 us  [local(): lax.all_to_all(pair_mix_re, 'row', split_axis=1, concat_axis=2, tiled=True)]
    dot_general x2 -> x4, matrix products: 2.21 us -> 4.44 us  [row_product(): jnp.einsum('rn,cnj->crj', phase, series, preferred_element_type=jnp.float32)]
    unnamed x2 -> x0, matrix products: 2.21 us -> none
    unnamed x19 -> x26, local copies, waits for them, and re-layouts: 8.34 us -> 7.81 us
  transfers between devices with their start and end apart: 5 -> 11, of which waited for: 4 -> 3; matrix products, arithmetic and copies ran while one was open for 6% -> 12% of each run, Pallas kernels for 0% -> 0%
where the time goes in v1:
time: 118 us; the launch traced here: 117 us
  blocking collectives  33 us (28%)
  starting transfers between devices  31.7 us (27%)
  local copies, waits for them, and re-layouts  20.9 us (18%)
  waiting for transfers between devices  17.1 us (14%)
  matrix products  13.7 us (12%)
    ppermute x7, starting transfers between devices, groups_create(): lax.ppermute(a_next, axis_name, [(c, c ^ h) for c in range(everything)])  12.9 us
    all_to_all x1, blocking collectives, local(): lax.all_to_all(pair_out, 'row', split_axis=1, concat_axis=2, tiled=True)  9.29 us
    dot_general x8, matrix products, column_product(): jnp.einsum('crn,nk->crk', series, phase, preferred_element_type=jnp.float32)  9.27 us
    dynamic_update_slice x8, local copies, waits for them, and re-layouts, groups_create(): lax.dynamic_update_slice_in_dim(y1, a_next, (mid_arr ^ h) * tmp, axis=1)  8.64 us
    unnamed x26, local copies, waits for them, and re-layouts  7.81 us
    all_to_all x1, waiting for transfers between devices, local(): lax.all_to_all(unwound_re, 'row', split_axis=2, concat_axis=1, tiled=True)  6.07 us
    all_gather x1, blocking collectives, local(): lax.all_gather(mixed_re, 'col', axis=2, tiled=True)  5.99 us
    all_to_all x1, starting transfers between devices, local(): lax.all_to_all(pair_mix_re, 'row', split_axis=1, concat_axis=2, tiled=True)  5.95 us
  transfers between devices with their start and end apart: 11, of which 3 were waited for; matrix products, arithmetic and copies ran while one was open for 12% of the time, Pallas kernels for 0%

profile of v1, /device:TPU:0, one launch (start us, length us, event | category | flops | bytes accessed | tf_op | source)
XLA Modules:
  0.0 117.2 jit_solution(959052607926505279)
XLA Ops:
  0.0 0.8 copy-done
  1.2 3.1 %collective-permute-start = (bf16[8,32,16]{1,2,0:T(8,128)(2,1)S(1)}, bf16[8,32,16]{1,2,0:T(8,128)(2,1)S(1)}, u32[]{:S(2)}, u32[]{:S(2)}) collective-permute-start(bf16[8,32,16]{1,2,0:T(8,128)(2,1)S(1)} %copy.62), channel_id=1, source_target_pairs={{0,4},{4,0},{8,12},{12,8},{16,20},{20,16},{24,28},{28,24},{1,5},{5... | collective-permute-start | bytes 24584 | tf_op jit(solution)/shard_map/ppermute | solution.py:19
  4.3 1.6 %collective-permute-start.1 = (bf16[8,32,16]{1,2,0:T(8,128)(2,1)S(1)}, bf16[8,32,16]{1,2,0:T(8,128)(2,1)S(1)}, u32[]{:S(2)}, u32[]{:S(2)}) collective-permute-start(bf16[8,32,16]{1,2,0:T(8,128)(2,1)S(1)} %copy.63), channel_id=1, source_target_pairs={{0,8},{4,12},{8,0},{12,4},{16,24},{20,28},{24,16},{28,20},{1,9},{5... | collective-permute-start | bytes 24584 | tf_op jit(solution)/shard_map/ppermute | solution.py:19
  6.2 3.0 %collective-permute-start.3 = (bf16[8,32,16]{1,2,0:T(8,128)(2,1)S(1)}, bf16[8,32,16]{1,2,0:T(8,128)(2,1)S(1)}, u32[]{:S(2)}, u32[]{:S(2)}) collective-permute-start(bf16[8,32,16]{1,2,0:T(8,128)(2,1)S(1)} %copy.65), channel_id=1, source_target_pairs={{0,16},{4,20},{8,24},{12,28},{16,0},{20,4},{24,8},{28,12},{1,17},{... | collective-permute-start | bytes 24584 | tf_op jit(solution)/shard_map/ppermute | solution.py:19
  9.3 1.4 %collective-permute-start.4 = (bf16[8,32,16]{1,2,0:T(8,128)(2,1)S(1)}, bf16[8,32,16]{1,2,0:T(8,128)(2,1)S(1)}, u32[]{:S(2)}, u32[]{:S(2)}) collective-permute-start(bf16[8,32,16]{1,2,0:T(8,128)(2,1)S(1)} %copy.66), channel_id=1, source_target_pairs={{0,20},{4,16},{8,28},{12,24},{16,4},{20,0},{24,12},{28,8},{1,21},{... | collective-permute-start | bytes 24584 | tf_op jit(solution)/shard_map/ppermute | solution.py:19
  11.1 3.7 %collective-permute-start.5 = (bf16[8,32,16]{1,2,0:T(8,128)(2,1)S(1)}, bf16[8,32,16]{1,2,0:T(8,128)(2,1)S(1)}, u32[]{:S(2)}, u32[]{:S(2)}) collective-permute-start(bf16[8,32,16]{1,2,0:T(8,128)(2,1)S(1)} %copy.67), channel_id=1, source_target_pairs={{0,24},{4,28},{8,16},{12,20},{16,8},{20,12},{24,0},{28,4},{1,25},{... | collective-permute-start | bytes 24584 | tf_op jit(solution)/shard_map/ppermute | solution.py:19
  15.2 1.4 %dynamic_update_slice.25 = bf16[8,256,16]{1,2,0:T(8,128)(2,1)S(1)} dynamic-update-slice(bf16[8,256,16]{1,2,0:T(8,128)(2,1)S(1)} %dynamic_update_slice.24, bf16[8,32,16]{1,2,0:T(8,128)(2,1)S(1)} %collective-permute-done, s32[]{:T(128)} %constant.72.clone.1, s32[]{:T(128)S(6)} %select_n.98, s32[]{:T(128)} %constant.72.clone.1) | dynamic-update-slice | bytes 16388 | tf_op jit(solution)/shard_map/dynamic_update_slice | solution.py:20
  16.6 1.4 %dynamic_update_slice.26 = bf16[8,256,16]{1,2,0:T(8,128)(2,1)S(1)} dynamic-update-slice(bf16[8,256,16]{1,2,0:T(8,128)(2,1)S(1)} %dynamic_update_slice.25, bf16[8,32,16]{1,2,0:T(8,128)(2,1)S(1)} %collective-permute-done.1, s32[]{:T(128)} %constant.72.clone.1, s32[]{:T(128)S(6)} %select_n.100, s32[]{:T(128)} %constant.72.clone.1) | dynamic-update-slice | bytes 16388 | tf_op jit(solution)/shard_map/dynamic_update_slice | solution.py:20
  18.0 1.4 %dynamic_update_slice.27 = bf16[8,256,16]{1,2,0:T(8,128)(2,1)S(1)} dynamic-update-slice(bf16[8,256,16]{1,2,0:T(8,128)(2,1)S(1)} %dynamic_update_slice.26, bf16[8,32,16]{1,2,0:T(8,128)(2,1)S(1)} %collective-permute-done.2, s32[]{:T(128)} %constant.72.clone.1, s32[]{:T(128)S(6)} %select_n.102, s32[]{:T(128)} %constant.72.clone.1) | dynamic-update-slice | bytes 16388 | tf_op jit(solution)/shard_map/dynamic_update_slice | solution.py:20
  19.6 1.3 %dynamic_update_slice.29 = bf16[8,256,16]{1,2,0:T(8,128)(2,1)S(1)} dynamic-update-slice(bf16[8,256,16]{1,2,0:T(8,128)(2,1)S(1)} %dynamic_update_slice.28, bf16[8,32,16]{1,2,0:T(8,128)(2,1)S(1)} %collective-permute-done.4, s32[]{:T(128)} %constant.72.clone.1, s32[]{:T(128)S(6)} %select_n.106, s32[]{:T(128)} %constant.72.clone.1) | dynamic-update-slice | bytes 16388 | tf_op jit(solution)/shard_map/dynamic_update_slice | solution.py:20
  21.0 1.3 %dynamic_update_slice.30 = bf16[8,256,16]{1,2,0:T(8,128)(2,1)S(1)} dynamic-update-slice(bf16[8,256,16]{1,2,0:T(8,128)(2,1)S(1)} %dynamic_update_slice.29, bf16[8,32,16]{1,2,0:T(8,128)(2,1)S(1)} %collective-permute-done.5, s32[]{:T(128)} %constant.72.clone.1, s32[]{:T(128)S(6)} %select_n.108, s32[]{:T(128)} %constant.72.clone.1) | dynamic-update-slice | bytes 16388 | tf_op jit(solution)/shard_map/dynamic_update_slice | solution.py:20
  22.4 1.3 %dynamic_update_slice.31 = bf16[8,256,16]{1,2,0:T(8,128)(2,1)S(1)} dynamic-update-slice(bf16[8,256,16]{1,2,0:T(8,128)(2,1)S(1)} %dynamic_update_slice.30, bf16[8,32,16]{1,2,0:T(8,128)(2,1)S(1)} %collective-permute-done.6, s32[]{:T(128)} %constant.72.clone.1, s32[]{:T(128)S(6)} %select_n.110, s32[]{:T(128)} %constant.72.clone.1) | dynamic-update-slice | bytes 16388 | tf_op jit(solution)/shard_map/dynamic_update_slice | solution.py:20
  23.7 1.1 convolution_bitcast_fusion.1
  24.8 1.1 add_convert_fusion.2
  26.3 1.2 %reshape.138 = bf16[8,2,2048]{2,1,0:T(2,128)(2,1)} reshape(bf16[256,8,16]{2,1,0:T(8,128)(2,1)S(1)} %bitcast.84) | data formatting | bytes 131072
  27.4 6.0 %all-to-all-start = ((bf16[8,2,2048]{2,1,0:T(2,128)(2,1)}), bf16[8,2,2048]{2,1,0:T(2,128)(2,1)S(1)}, u32[]{:S(2)}, u32[]{:S(2)}) async-start(bf16[8,2,2048]{2,1,0:T(2,128)(2,1)} %reshape.138), calls=%async_computation | async-start | bytes 131072 | tf_op jit(solution)/shard_map/all_to_all | solution.py:67
  33.9 1.2 %reshape.140 = bf16[8,2,2048]{2,1,0:T(2,128)(2,1)} reshape(bf16[256,8,16]{2,1,0:T(8,128)(2,1)S(1)} %bitcast.85) | data formatting | bytes 131072
  35.0 5.3 %all-to-all-done = bf16[8,2,2048]{2,1,0:T(2,128)(2,1)S(1)} async-done(((bf16[8,2,2048]{2,1,0:T(2,128)(2,1)}), bf16[8,2,2048]{2,1,0:T(2,128)(2,1)S(1)}, u32[]{:S(2)}, u32[]{:S(2)}) %all-to-all-start) | async-done | bytes 65568 | tf_op jit(solution)/shard_map/all_to_all | solution.py:67
  40.3 3.3 %all-to-all-start.1 = ((bf16[8,2,2048]{2,1,0:T(2,128)(2,1)}), bf16[8,2,2048]{2,1,0:T(2,128)(2,1)S(1)}, u32[]{:S(2)}, u32[]{:S(2)}) async-start(bf16[8,2,2048]{2,1,0:T(2,128)(2,1)} %reshape.140), calls=%async_computation.1 | async-start | bytes 131072 | tf_op jit(solution)/shard_map/all_to_all | solution.py:68
  43.7 0.4 reshape.139
  44.0 0.4 copy.45
  44.6 6.0 %all_gather.12 = bf16[8,32,512]{2,1,0:T(8,128)(2,1)S(1)} all-gather(bf16[8,32,128]{2,1,0:T(8,128)(2,1)S(1)} %copy.46), channel_id=1, replica_groups=mesh['row'=8,'col'=4] {'col'}, dimensions={2}, use_global_device_ids=true | all-gather | bytes 327680 | tf_op jit(solution)/shard_map/all_gather | solution.py:71
  50.6 1.2 fusion.24
  51.7 1.2 fusion.32
  52.9 0.4 reshape.141
  53.3 0.4 copy.48
  53.8 5.9 %all_gather.13 = bf16[8,32,512]{2,1,0:T(8,128)(2,1)S(1)} all-gather(bf16[8,32,128]{2,1,0:T(8,128)(2,1)S(1)} %copy.49), channel_id=1, replica_groups=mesh['row'=8,'col'=4] {'col'}, dimensions={2}, use_global_device_ids=true | all-gather | bytes 327680 | tf_op jit(solution)/shard_map/all_gather | solution.py:72
  59.7 1.2 convolution_add_fusion.1
  60.9 1.2 %fusion.15 = (bf16[8,32,128]{2,1,0:T(8,128)(2,1)S(1)}, bf16[8,32,128]{2,1,0:T(8,128)(2,1)S(1)}) fusion(bf16[8,32,128]{2,1,0:T(8,128)(2,1)S(1)} %copy-done.1, f32[8,32,128]{2,1,0:T(8,128)S(1)} %convolution_add_fusion.1, bf16[8,32,128]{2,1,0:T(8,128)(2,1)S(1)} %copy-done.2, f32[8,32,128]{2,1,0:T(8,128)S(1)} %fusion.32, ...), kind=kOutput, calls=%fused_computation.36 | convolution fusion | flops 34897920 | bytes 786944 | tf_op jit(solution)/shard_map/crn,nk->crk/dot_general | solution.py:37
  62.1 5.9 %all_gather.14 = bf16[8,32,512]{2,1,0:T(8,128)(2,1)S(1)} all-gather(bf16[8,32,128]{2,1,0:T(8,128)(2,1)S(1)} %get-tuple-element.5), channel_id=1, replica_groups=mesh['row'=8,'col'=4] {'col'}, dimensions={2}, use_global_device_ids=true | all-gather | bytes 327680 | tf_op jit(solution)/shard_map/all_gather | solution.py:84
  68.0 1.2 fusion.29
  69.1 5.9 %all_gather.15 = bf16[8,32,512]{2,1,0:T(8,128)(2,1)S(1)} all-gather(bf16[8,32,128]{2,1,0:T(8,128)(2,1)S(1)} %get-tuple-element.6), channel_id=1, replica_groups=mesh['row'=8,'col'=4] {'col'}, dimensions={2}, use_global_device_ids=true | all-gather | bytes 327680 | tf_op jit(solution)/shard_map/all_gather | solution.py:85
  75.1 1.2 fusion.27
  76.2 1.2 convolution_subtract_fusion
  77.4 1.2 %subtract_convert_fusion = (bf16[8,32,128]{2,1,0:T(8,128)(2,1)S(1)}, bf16[8,32,128]{2,1,0:T(8,128)(2,1)S(1)}) fusion(f32[8,32,128]{2,1,0:T(8,128)S(1)} %convolution_subtract_fusion, f32[32,128]{1,0:T(8,128)S(1)} %get-tuple-element.20, f32[32,128]{1,0:T(8,128)S(1)} %get-tuple-element.19, f32[8,32,128]{2,1,0:T(8,128)S(1)} %fusion.29, ...), kind=kOutput, calls=%fused_computation.44 | convolution fusion | flops 34832384 | bytes 688640 | tf_op jit(solution)/shard_map/crn,nk->crk/dot_general | solution.py:37
  78.8 0.9 reshape.144
  79.7 5.9 %all-to-all-start.3 = ((bf16[8,2,2048]{2,1,0:T(2,128)(2,1)}), bf16[8,2,2048]{2,1,0:T(2,128)(2,1)S(1)}, u32[]{:S(2)}, u32[]{:S(2)}) async-start(bf16[8,2,2048]{2,1,0:T(2,128)(2,1)} %reshape.144), calls=%async_computation.3 | async-start | bytes 131072 | tf_op jit(solution)/shard_map/all_to_all | solution.py:96
  85.8 0.9 reshape.142
  86.7 5.8 %all-to-all-done.3 = bf16[8,2,2048]{2,1,0:T(2,128)(2,1)S(1)} async-done(((bf16[8,2,2048]{2,1,0:T(2,128)(2,1)}), bf16[8,2,2048]{2,1,0:T(2,128)(2,1)S(1)}, u32[]{:S(2)}, u32[]{:S(2)}) %all-to-all-start.3) | async-done | bytes 65568 | tf_op jit(solution)/shard_map/all_to_all | solution.py:96
  92.5 3.6 %all-to-all-start.2 = ((bf16[8,2,2048]{2,1,0:T(2,128)(2,1)}), bf16[8,2,2048]{2,1,0:T(2,128)(2,1)S(1)}, u32[]{:S(2)}, u32[]{:S(2)}) async-start(bf16[8,2,2048]{2,1,0:T(2,128)(2,1)} %reshape.142), calls=%async_computation.2 | async-start | bytes 131072 | tf_op jit(solution)/shard_map/all_to_all | solution.py:95
  96.6 6.1 %all-to-all-done.2 = bf16[8,2,2048]{2,1,0:T(2,128)(2,1)S(1)} async-done(((bf16[8,2,2048]{2,1,0:T(2,128)(2,1)}), bf16[8,2,2048]{2,1,0:T(2,128)(2,1)S(1)}, u32[]{:S(2)}, u32[]{:S(2)}) %all-to-all-start.2) | async-done | bytes 65568 | tf_op jit(solution)/shard_map/all_to_all | solution.py:95
  103.3 1.1 fusion.38
  104.4 1.1 add_convert_fusion
  105.8 0.5 reshape.146
  106.4 9.3 %all_to_all.90 = bf16[8,2,2048]{2,1,0:T(2,128)(2,1)S(1)} all-to-all(bf16[8,2,2048]{2,1,0:T(2,128)(2,1)S(1)} %reshape.146), channel_id=1, replica_groups=mesh['row'=8,'col'=4] {'row'}, dimensions={0} | all-to-all | bytes 131072 | tf_op jit(solution)/shard_map/all_to_all | solution.py:102
  115.7 0.4 reshape.147
  116.0 0.4 copy.57
  116.4 0.8 copy.58
  (47 shorter events, 4.6 us)
Async XLA Ops:
  0.0 0.8 copy-start
  1.2 9.9 %collective-permute-start = (bf16[8,32,16]{1,2,0:T(8,128)(2,1)S(1)}, bf16[8,32,16]{1,2,0:T(8,128)(2,1)S(1)}, u32[]{:S(2)}, u32[]{:S(2)}) collective-permute-start(bf16[8,32,16]{1,2,0:T(8,128)(2,1)S(1)} %copy.62), channel_id=1, source_target_pairs={{0,4},{4,0},{8,12},{12,8},{16,20},{20,16},{24,28},{28,24},{1,5},{5... | collective-permute-start | bytes 24584 | tf_op jit(solution)/shard_map/ppermute | solution.py:19
  4.3 10.4 %collective-permute-start.1 = (bf16[8,32,16]{1,2,0:T(8,128)(2,1)S(1)}, bf16[8,32,16]{1,2,0:T(8,128)(2,1)S(1)}, u32[]{:S(2)}, u32[]{:S(2)}) collective-permute-start(bf16[8,32,16]{1,2,0:T(8,128)(2,1)S(1)} %copy.63), channel_id=1, source_target_pairs={{0,8},{4,12},{8,0},{12,4},{16,24},{20,28},{24,16},{28,20},{1,9},{5... | collective-permute-start | bytes 24584 | tf_op jit(solution)/shard_map/ppermute | solution.py:19
  6.0 11.9 %collective-permute-start.2 = (bf16[8,32,16]{1,2,0:T(8,128)(2,1)S(1)}, bf16[8,32,16]{1,2,0:T(8,128)(2,1)S(1)}, u32[]{:S(2)}, u32[]{:S(2)}) collective-permute-start(bf16[8,32,16]{1,2,0:T(8,128)(2,1)S(1)} %copy.64), channel_id=1, source_target_pairs={{0,12},{4,8},{8,4},{12,0},{16,28},{20,24},{24,20},{28,16},{1,13},{... | collective-permute-start | bytes 24584 | tf_op jit(solution)/shard_map/ppermute | solution.py:19
  6.2 13.1 %collective-permute-start.3 = (bf16[8,32,16]{1,2,0:T(8,128)(2,1)S(1)}, bf16[8,32,16]{1,2,0:T(8,128)(2,1)S(1)}, u32[]{:S(2)}, u32[]{:S(2)}) collective-permute-start(bf16[8,32,16]{1,2,0:T(8,128)(2,1)S(1)} %copy.65), channel_id=1, source_target_pairs={{0,16},{4,20},{8,24},{12,28},{16,0},{20,4},{24,8},{28,12},{1,17},{... | collective-permute-start | bytes 24584 | tf_op jit(solution)/shard_map/ppermute | solution.py:19
  9.3 10.3 %collective-permute-start.4 = (bf16[8,32,16]{1,2,0:T(8,128)(2,1)S(1)}, bf16[8,32,16]{1,2,0:T(8,128)(2,1)S(1)}, u32[]{:S(2)}, u32[]{:S(2)}) collective-permute-start(bf16[8,32,16]{1,2,0:T(8,128)(2,1)S(1)} %copy.66), channel_id=1, source_target_pairs={{0,20},{4,16},{8,28},{12,24},{16,4},{20,0},{24,12},{28,8},{1,21},{... | collective-permute-start | bytes 24584 | tf_op jit(solution)/shard_map/ppermute | solution.py:19
  11.1 9.9 %collective-permute-start.5 = (bf16[8,32,16]{1,2,0:T(8,128)(2,1)S(1)}, bf16[8,32,16]{1,2,0:T(8,128)(2,1)S(1)}, u32[]{:S(2)}, u32[]{:S(2)}) collective-permute-start(bf16[8,32,16]{1,2,0:T(8,128)(2,1)S(1)} %copy.67), channel_id=1, source_target_pairs={{0,24},{4,28},{8,16},{12,20},{16,8},{20,12},{24,0},{28,4},{1,25},{... | collective-permute-start | bytes 24584 | tf_op jit(solution)/shard_map/ppermute | solution.py:19
  14.8 7.6 %collective-permute-start.6 = (bf16[8,32,16]{1,2,0:T(8,128)(2,1)S(1)}, bf16[8,32,16]{1,2,0:T(8,128)(2,1)S(1)}, u32[]{:S(2)}, u32[]{:S(2)}) collective-permute-start(bf16[8,32,16]{1,2,0:T(8,128)(2,1)S(1)} %copy.68), channel_id=1, source_target_pairs={{0,28},{4,24},{8,20},{12,16},{16,12},{20,8},{24,4},{28,0},{1,29},{... | collective-permute-start | bytes 24584 | tf_op jit(solution)/shard_map/ppermute | solution.py:19
  27.4 12.9 %all-to-all-start = ((bf16[8,2,2048]{2,1,0:T(2,128)(2,1)}), bf16[8,2,2048]{2,1,0:T(2,128)(2,1)S(1)}, u32[]{:S(2)}, u32[]{:S(2)}) async-start(bf16[8,2,2048]{2,1,0:T(2,128)(2,1)} %reshape.138), calls=%async_computation | async-start | bytes 131072 | tf_op jit(solution)/shard_map/all_to_all | solution.py:67
  40.3 12.6 %all-to-all-start.1 = ((bf16[8,2,2048]{2,1,0:T(2,128)(2,1)}), bf16[8,2,2048]{2,1,0:T(2,128)(2,1)S(1)}, u32[]{:S(2)}, u32[]{:S(2)}) async-start(bf16[8,2,2048]{2,1,0:T(2,128)(2,1)} %reshape.140), calls=%async_computation.1 | async-start | bytes 131072 | tf_op jit(solution)/shard_map/all_to_all | solution.py:68
  59.7 1.2 copy-start.1
  59.7 1.2 %copy-start.2 = (bf16[8,32,128]{2,1,0:T(8,128)(2,1)S(1)}, bf16[8,32,128]{2,1,0:T(8,128)(2,1)}, u32[]{:S(2)}) copy-start(bf16[8,32,128]{2,1,0:T(8,128)(2,1)} %param.6) | copy-start | bytes 196612
  79.7 12.8 %all-to-all-start.3 = ((bf16[8,2,2048]{2,1,0:T(2,128)(2,1)}), bf16[8,2,2048]{2,1,0:T(2,128)(2,1)S(1)}, u32[]{:S(2)}, u32[]{:S(2)}) async-start(bf16[8,2,2048]{2,1,0:T(2,128)(2,1)} %reshape.144), calls=%async_computation.3 | async-start | bytes 131072 | tf_op jit(solution)/shard_map/all_to_all | solution.py:96
  92.5 10.2 %all-to-all-start.2 = ((bf16[8,2,2048]{2,1,0:T(2,128)(2,1)}), bf16[8,2,2048]{2,1,0:T(2,128)(2,1)S(1)}, u32[]{:S(2)}, u32[]{:S(2)}) async-start(bf16[8,2,2048]{2,1,0:T(2,128)(2,1)} %reshape.142), calls=%async_computation.2 | async-start | bytes 131072 | tf_op jit(solution)/shard_map/all_to_all | solution.py:95
  103.3 1.1 copy-start.3
